TPU v7x, 128 devices: a whole 4x4x4 slice. The times are simulated.
128 devices in a mesh: dp: 4 (over z), latent: 32 (over x, y, core).
Axes of the slice: x: 4, y: 4, z: 4, core: 2. Of those that a mesh axis runs over, the one named last changes fastest.
Arguments:
- acts: bfloat16 [640, 8192], P(('dp', 'latent')), may hold values from -6 to 6
- chat_len: int32 [128], P(('dp', 'latent')), may hold values from 1 to 5, as said below
- group_of: int32 [640, 1], P(('dp', 'latent')), may hold values from 0 to 4; in each aligned block of 5 rows (0 to 4, 5 to 9, ...) no two rows name the same one
- w_enc: bfloat16 [2, 4096, 16384], P(None, None, 'latent'), may hold values from -0.0625 to 0.0625
- b_enc: float32 [16384], P('latent'), may hold values from -3 to 3
- w_dec: bfloat16 [16384, 8192], P('latent'), may hold values from -0.046875 to 0.046875
- b_dec: float32 [2, 4096], replicated, may hold values from -3 to 3
Outputs:
- grad_enc: bfloat16 [2, 4096, 16384], P(None, 'dp', 'latent')
- grad_dec: bfloat16 [16384, 8192], P('latent', 'dp')
- loss: float32 [], replicated
Inputs may be any that keep to these rules, and one draw needn't show every extreme that they name: `chat_len`: the last serving shard harvests all 5 rows. `group_of`: among the 5 row slots of each serving shard every value 0 to 4 appears exactly once.
All inputs are finite; a program needn't handle non-finite values.
Results may differ from a plain program's by a relative error of at most 0.02.
Values may be sent and summed in bfloat16 or wider, within the bound.
No kernel may reach another device: no remote copies, remote signals or barrier semaphores. Data moves between devices by JAX's collectives and lax.ppermute only.
A program may use at most 128 MiB of HBM per device.

v0:
```python
import jax
import jax.numpy as jnp
from jax import lax
from jax.sharding import PartitionSpec as P

sparsity_weight = 1.0
loss_scale = 8.0
norm_eps = 1e-06


def shards(acts, chat_len, group_of, w_enc, b_enc, w_dec, b_dec):
    groups = lax.axis_size("dp")
    slots = acts.shape[0]
    width = acts.shape[1]
    half = width // 2
    local_latents = w_enc.shape[2]
    capacity = slots // (groups + 1)
    slot_ids = jnp.arange(slots, dtype=jnp.int32)
    alive = (slot_ids < chat_len[0]).astype(jnp.float32)
    order = jnp.argsort(group_of[:, 0], stable=True)[: groups * capacity]
    own_count = jnp.sum(alive[order])
    outgoing = acts[order].reshape(groups, capacity, width)
    out_mask = alive[order].reshape(groups, capacity).astype(jnp.bfloat16)
    received, recv_mask = (
        lax.all_to_all(outgoing, "dp", split_axis=0, concat_axis=0, tiled=True),
        lax.all_to_all(out_mask, "dp", split_axis=0, concat_axis=0, tiled=True),
    )
    member_rows, member_mask = (
        lax.all_gather(received, "latent", axis=0, tiled=True),
        lax.all_gather(recv_mask, "latent", axis=0, tiled=True),
    )
    xg = member_rows.reshape(-1, width)
    maskg = member_mask.reshape(-1).astype(jnp.float32)
    total_rows = xg.shape[0]
    share_rows = total_rows // lax.axis_size("latent")
    first_row = lax.axis_index("latent") * share_rows
    wenc_flat = w_enc.reshape(width, local_latents)
    squares_dec = jnp.square(w_dec.astype(jnp.float32))
    norm_base = jnp.sqrt(jnp.sum(squares_dec[:, :half], axis=1) + norm_eps)
    norm_inst = jnp.sqrt(jnp.sum(squares_dec[:, half:], axis=1) + norm_eps)
    norm_sum = norm_base + norm_inst
    column_ids = jnp.arange(width, dtype=jnp.int32)
    bias_row = b_dec.reshape(width)
    pre = jnp.dot(xg, wenc_flat, preferred_element_type=jnp.float32) + b_enc[None, :]
    act = jnp.maximum(pre, 0.0)
    feats = act * act
    feats16 = feats.astype(jnp.bfloat16)
    partial_value = jnp.dot(feats16, w_dec, preferred_element_type=jnp.float32)
    recon = lax.psum(partial_value.astype(jnp.bfloat16), "latent").astype(jnp.float32)
    err = (recon + bias_row[None, :] - xg.astype(jnp.float32)) * maskg[:, None]
    err16 = err.astype(jnp.bfloat16)
    err_share = lax.dynamic_slice_in_dim(err, first_row, share_rows, 0)
    square_sum = jnp.sum(err_share * err_share)
    feat_sum = jnp.sum(feats * maskg[:, None], axis=0)
    local_loss = square_sum + sparsity_weight * jnp.sum(feat_sum * norm_sum)
    dfeat = 2.0 * lax.dot_general(
        err16, w_dec, (((1,), (1,)), ((), ())), preferred_element_type=jnp.float32
    )
    dfeat = dfeat + sparsity_weight * maskg[:, None] * norm_sum[None, :]
    dpre16 = (dfeat * 2.0 * act).astype(jnp.bfloat16)
    enc_term = lax.dot_general(
        xg, dpre16, (((0,), (0,)), ((), ())), preferred_element_type=jnp.float32
    )
    enc_term = enc_term.reshape(2, half, local_latents)
    dec_term = 2.0 * lax.dot_general(
        feats16, err16, (((0,), (0,)), ((), ())), preferred_element_type=jnp.float32
    )
    scale = jnp.where(
        column_ids[None, :] < half, (feat_sum / norm_base)[:, None], (feat_sum / norm_inst)[:, None]
    )
    dec_term = dec_term + sparsity_weight * scale * w_dec.astype(jnp.float32)
    enc_total = lax.psum_scatter(
        enc_term.astype(jnp.bfloat16), "dp", scatter_dimension=1, tiled=True
    ).astype(jnp.float32)
    dec_total = lax.psum_scatter(
        dec_term.astype(jnp.bfloat16), "dp", scatter_dimension=1, tiled=True
    ).astype(jnp.float32)
    total, count = lax.psum((local_loss, own_count), ("dp", "latent"))
    factor = loss_scale / count
    grad_enc = (enc_total * factor).astype(jnp.bfloat16)
    grad_dec = (dec_total * factor).astype(jnp.bfloat16)
    loss = total / (count * width)
    return (grad_enc, grad_dec, loss)


def solution(mesh):
    return jax.shard_map(
        shards,
        mesh=mesh,
        in_specs=(
            P(("dp", "latent"), None),
            P(("dp", "latent")),
            P(("dp", "latent"), None),
            P(None, None, "latent"),
            P("latent"),
            P("latent", None),
            P(),
        ),
        out_specs=(P(None, "dp", "latent"), P("latent", "dp"), P()),
        check_vma=False,
    )
```

profile of v0, /device:TPU:1, one launch (start us, length us, event | category | flops | bytes accessed | tf_op | source)
XLA Modules:
  0.0 414.3 jit_solution(3964806186658669848)
XLA Ops:
  7.2 0.0 copy-start
  7.2 0.0 all-gather.3.cloned.1.call-start
  7.2 1.6 sort.17
  8.9 0.0 copy-done
  8.9 0.6 gather_fusion
  9.5 0.5 broadcast.57
  10.0 0.7 reduce.2
  10.7 0.1 reshape.95
  10.8 10.1 %all_to_all.14 = bf16[4,2,4096]{2,1,0:T(2,128)(2,1)S(1)} all-to-all(bf16[4,2,4096]{2,1,0:T(2,128)(2,1)S(1)} %reshape.95), channel_id=1, replica_groups=mesh['dp'=4,'latent'=32] {'dp'}, dimensions={0} | all-to-all | bytes 131072 | tf_op jit(solution)/shard_map/all_to_all | solution.py:25
  20.9 0.7 reshape.96
  21.6 0.0 all-gather.3.cloned.1.call-update
  22.3 0.6 gather_fusion.1
  23.0 0.6 fusion.25
  23.6 0.7 copy.17
  24.3 3.2 all-to-all-start.1
  27.5 0.0 all-reduce.4.cloned.1.call-start
  27.5 1.3 dynamic-slice
  29.6 1.9 all-to-all-done.1
  31.5 0.1 reduce.1
  31.6 0.2 dynamic-update-slice
  31.8 65.9 %all-reduce = bf16[128]{0:T(256)(128)(2,1)S(1)} all-reduce(bf16[128]{0:T(256)(128)(2,1)S(1)} %dynamic-update-slice), channel_id=2, replica_groups=mesh['dp'=4,'latent'=32] {'latent'}, use_global_device_ids=true, to_apply=%add | all-reduce | flops 128 | bytes 512
  97.7 0.0 all-gather.3.cloned.1.call-done
  97.8 7.3 %multiply_reduce_fusion = (f32[512]{0:T(512)S(1)}, f32[128,512]{1,0:T(8,128)S(1)}) fusion(f32[128]{0:T(128)S(1)} %mul.102, f32[512]{0:T(512)} %param.11, bf16[8192,512]{1,0:T(8,128)(2,1)} %bitcast.33, bf16[128,1,8192]{2,1,0:T(2,128)(2,1)} %all-gather.3.cloned.1.call-done), kind=kOutput, calls=%fused_computation.26 | convolution fusion | flops 1074068992 | bytes 10752512 | tf_op jit(solution)/shard_map/dot_general | solution.py:44
  105.1 6.0 %convolution_convert_fusion = bf16[128,8192]{1,0:T(8,128)(2,1)} fusion(bf16[512,8192]{1,0:T(8,128)(2,1)} %param.12, f32[128,512]{1,0:T(8,128)S(1)} %get-tuple-element.16), kind=kOutput, calls=%fused_computation.6 | convolution fusion | flops 1074921472 | bytes 10747904 | tf_op jit(solution)/shard_map/dot_general | solution.py:48
  111.0 0.0 all-reduce.4.cloned.1.call-update
  111.1 0.0 copy-start.2
  111.1 0.2 reduce-scatter.3.cloned.1.call-start
  111.3 11.3 %convert_multiply_fusion.1 = f32[512,8192]{1,0:T(8,128)} fusion(bf16[512,8192]{1,0:T(8,128)(2,1)} %param.12), kind=kLoop, calls=%fused_computation.3 | loop fusion | flops 8388608 | bytes 25165824 | tf_op jit(solution)/shard_map/square | solution.py:38
  122.6 0.0 copy-done.2
  122.6 6.5 %slice_reduce_fusion.1 = (f32[512]{0:T(512)S(1)}, f32[512]{0:T(512)S(1)}) fusion(f32[512,8192]{1,0:T(8,128)} %convert_multiply_fusion.1), kind=kLoop, calls=%fused_computation.8 | loop fusion | flops 4193280 | bytes 16781312 | tf_op jit(solution)/shard_map/reduce_sum | solution.py:39
  129.2 8.8 %copy.19 = bf16[128,1,8192]{0,2,1:T(8,128)(2,1)S(1)} copy(bf16[128,1,8192]{2,1,0:T(2,128)(2,1)} %all-gather.3.cloned.1.call-done) | data formatting | bytes 4194304 | tf_op jit(solution)/shard_map/dot_general | solution.py:61
  138.0 0.6 multiply_reduce_fusion.2
  138.6 75.9 %all-reduce.4.cloned.1.call-done = bf16[128,8192]{1,0:T(8,128)(2,1)} async-done(((bf16[128,8192]{1,0:T(8,128)(2,1)}), bf16[128,8192]{1,0:T(8,128)(2,1)}) %all-reduce.4.cloned.1.call-update) | async-done | bytes 2097168 | tf_op jit(solution)/shard_map/psum | solution.py:49
  214.5 8.7 %subtract_multiply_fusion = f32[128,8192]{1,0:T(8,128)} fusion(bf16[128,8192]{1,0:T(8,128)(2,1)} %all-reduce.4.cloned.1.call-done, f32[128]{0:T(128)S(1)} %mul.102, f32[8192]{0:T(1024)S(1)} %bitcast.36, bf16[128,1,8192]{2,1,0:T(2,128)(2,1)} %all-gather.3.cloned.1.call-done), kind=kLoop, calls=%fused_computation.12 | loop fusion | flops 5242880 | bytes 8421888 | tf_op jit(solution)/shard_map/mul | solution.py:50
  223.2 15.0 %convolution_convert_fusion.1 = bf16[2,4096,512]{2,1,0:T(8,128)(2,1)} fusion(bf16[2,4096,128]{2,1,0:T(8,128)(2,1)S(1)} %bitcast.34, f32[128,512]{1,0:T(8,128)S(1)} %get-tuple-element.16, bf16[512,8192]{1,0:T(8,128)(2,1)} %param.12, f32[128,8192]{1,0:T(8,128)} %subtract_multiply_fusion, f32[512]{0:T(512)S(1)} %get-tuple-element.10, f32[128]{0:T(128)S(1)} %mul.102), kind=kOutput, calls=%fused_computation.9 | convolution fusion | flops 2153119744 | bytes 23333376 | tf_op jit(solution)/shard_map/dot_general | solution.py:61
  238.2 0.0 reduce-scatter.3.cloned.1.call-update
  238.2 0.0 reduce-scatter.5.cloned.1.call-start
  238.3 9.8 %fusion.1 = bf16[512,8192]{1,0:T(8,128)(2,1)} fusion(bf16[512,8192]{1,0:T(8,128)(2,1)} %param.12, f32[512]{0:T(512)S(1)} %get-tuple-element.12, f32[512]{0:T(512)S(1)} %get-tuple-element.11, pred[8192]{0:T(1024)(128)(4,1)S(1)} %iota_compare_fusion, f32[128,8192]{1,0:T(8,128)} %subtract_multiply_fusion, f32[128,512]{1,0:T(8,128)S(1)} %get-tuple-element.16), kind=kOutput, calls=%fused_computation.5 | convolution fusion | flops 1100087296 | bytes 21245952 | tf_op jit(solution)/shard_map/dot_general | solution.py:65
  248.0 0.0 reduce-scatter.5.cloned.1.call-update
  248.1 1.6 multiply_reduce_fusion.1
  251.0 69.5 %all-reduce.1 = (f32[]{:T(128)}, f32[]{:T(128)}) all-reduce(f32[]{:T(128)} %get-tuple-element.13, f32[]{:T(128)S(6)} %add.86), channel_id=1, replica_groups=mesh['dp'=4,'latent'=32] {'dp','latent'}, use_global_device_ids=true, to_apply=%region_6.7 | all-reduce | flops 2 | bytes 16 | tf_op jit(solution)/shard_map/psum | solution.py:78
  321.8 0.0 copy-start.1
  322.5 0.0 reduce-scatter.3.cloned.1.call-done
  322.5 3.3 multiply_convert_fusion.1
  325.8 77.3 %reduce-scatter.5.cloned.1.call-done = bf16[512,2048]{1,0:T(8,128)(2,1)} async-done(((bf16[512,8192]{1,0:T(8,128)(2,1)}), bf16[512,2048]{1,0:T(8,128)(2,1)}) %reduce-scatter.5.cloned.1.call-update) | async-done | bytes 2097168 | tf_op jit(solution)/shard_map/reduce_scatter | solution.py:75
  403.2 3.4 multiply_convert_fusion
  406.6 0.0 copy-done.1
  (8 shorter events, 0.0 us)
Async XLA Ops:
  7.2 1.7 copy-start
  7.2 90.6 %all-gather.3.cloned.1.call-start = ((), (), s32[]{:S(2)}) async-start(), calls=%async_computation.4 | async-start | bytes 4325376 | tf_op jit(solution)/shard_map/all_gather | solution.py:29
  24.3 7.2 %all-to-all-start.1 = ((bf16[4,1,1]{2,1,0:T(2,128)(2,1)}), bf16[4,1,1]{2,1,0:T(2,128)(2,1)S(1)}, u32[]{:S(2)}, u32[]{:S(2)}) async-start(bf16[4,1,1]{2,1,0:T(2,128)(2,1)} %copy.17), calls=%async_computation.1 | async-start | bytes 4096 | tf_op jit(solution)/shard_map/all_to_all | solution.py:26
  27.5 187.0 %all-reduce.4.cloned.1.call-start = ((), (), s32[]{:S(2)}) async-start(), calls=%async_computation.5 | async-start | bytes 4194304 | tf_op jit(solution)/shard_map/psum | solution.py:49
  111.1 11.6 %copy-start.2 = (f32[2,4096]{1,0:T(2,128)S(1)}, f32[2,4096]{1,0:T(2,128)}, u32[]{:S(2)}) copy-start(f32[2,4096]{1,0:T(2,128)} %param.13) | copy-start | bytes 98308
  111.1 211.4 %reduce-scatter.3.cloned.1.call-start = ((), (), s32[]{:S(2)}) async-start(), calls=%async_computation.6 | async-start | bytes 10485760 | tf_op jit(solution)/shard_map/reduce_scatter | solution.py:72
  238.2 165.0 %reduce-scatter.5.cloned.1.call-start = ((), (), s32[]{:S(2)}) async-start(), calls=%async_computation.7 | async-start | bytes 10485760 | tf_op jit(solution)/shard_map/reduce_scatter | solution.py:75
  321.8 84.8 %copy-start.1 = (bf16[5,8192]{1,0:T(8,128)(2,1)S(1)}, bf16[5,8192]{1,0:T(8,128)(2,1)}, u32[]{:S(2)}) copy-start(bf16[5,8192]{1,0:T(8,128)(2,1)} %param.7) | copy-start | bytes 245764
Sparse Core Ops, SparseCore 0:
  21.8 47.3 all-gather.2
  111.2 103.2 all-reduce.3
  238.3 82.5 reduce-scatter.2
  323.2 79.8 reduce-scatter.4
where the time goes:
time: 415 us; the launch traced here: 414 us
  waiting for transfers between devices  155 us (37%)
  blocking collectives  145 us (35%)
  other arithmetic  38.6 us (9%)
  matrix products  38 us (9%)
  between operations  19.7 us (5%)
  local copies, waits for them, and re-layouts  13.6 us (3%)
    reduce_scatter x1, waiting for transfers between devices, shards(): lax.psum_scatter(dec_term.astype(jnp.bfloat16), 'dp', scatter_dimension=1...  77.3 us
    psum x1, waiting for transfers between devices, shards(): lax.psum(partial_value.astype(jnp.bfloat16), 'latent').astype(jnp.float32)  75.9 us
    psum x1, blocking collectives, shards(): total, count = lax.psum((local_loss, own_count), ('dp', 'latent'))  69.5 us
    unnamed x1, blocking collectives  65.9 us
    dot_general x1, matrix products, shards(): lax.dot_general(xg, dpre16, (((0,), (0,)), ((), ())), preferred_element_t...  15 us
    square x1, other arithmetic, shards(): squares_dec = jnp.square(w_dec.astype(jnp.float32))  11.3 us
    all_to_all x1, blocking collectives, shards(): lax.all_to_all(outgoing, 'dp', split_axis=0, concat_axis=0, tiled=True)  10.1 us
    dot_general x1, matrix products, shards(): lax.dot_general(feats16, err16, (((0,), (0,)), ((), ())), preferred_eleme...  9.77 us
  transfers between devices with their start and end apart: 5, of which 3 were waited for; matrix products, arithmetic and copies ran while one was open for 11% of the time, Pallas kernels for 0%

commit v1 on v0

--- a/solution.py
+++ b/solution.py
@@ -75,7 +75,13 @@
     dec_total = lax.psum_scatter(
         dec_term.astype(jnp.bfloat16), "dp", scatter_dimension=1, tiled=True
     ).astype(jnp.float32)
-    total, count = lax.psum((local_loss, own_count), ("dp", "latent"))
+
+    def register_frames(chunk):
+        for it in ("dp", "latent"):
+            chunk = lax.psum(chunk, it)
+        return chunk
+
+    total, count = register_frames((local_loss, own_count))
     factor = loss_scale / count
     grad_enc = (enc_total * factor).astype(jnp.bfloat16)
     grad_dec = (dec_total * factor).astype(jnp.bfloat16)

time: 415 us -> 414 us (level)
  waiting for transfers between devices: 155 us -> 148 us
  blocking collectives: 145 us -> 151 us
    reduce_scatter x1, waiting for transfers between devices: 77.3 us -> 70.3 us  [shards(): lax.psum_scatter(dec_term.astype(jnp.bfloat16), 'dp', scatter_dimension=1...]
    psum x1 -> x2, blocking collectives: 69.5 us -> 75.1 us  [register_frames(): chunk = lax.psum(chunk, it)]
where the time goes in v1:
time: 414 us; the launch traced here: 413 us
  blocking collectives  151 us (36%)
  waiting for transfers between devices  148 us (36%)
  other arithmetic  38.6 us (9%)
  matrix products  38 us (9%)
  between operations  19.7 us (5%)
  local copies, waits for them, and re-layouts  13.6 us (3%)
    psum x1, waiting for transfers between devices, shards(): lax.psum(partial_value.astype(jnp.bfloat16), 'latent').astype(jnp.float32)  75.9 us
    psum x2, blocking collectives, register_frames(): chunk = lax.psum(chunk, it)  75.1 us
    reduce_scatter x1, waiting for transfers between devices, shards(): lax.psum_scatter(dec_term.astype(jnp.bfloat16), 'dp', scatter_dimension=1...  70.3 us
    unnamed x1, blocking collectives  65.9 us
    dot_general x1, matrix products, shards(): lax.dot_general(xg, dpre16, (((0,), (0,)), ((), ())), preferred_element_t...  15 us
    square x1, other arithmetic, shards(): squares_dec = jnp.square(w_dec.astype(jnp.float32))  11.3 us
    all_to_all x1, blocking collectives, shards(): lax.all_to_all(outgoing, 'dp', split_axis=0, concat_axis=0, tiled=True)  10.1 us
    dot_general x1, matrix products, shards(): lax.dot_general(feats16, err16, (((0,), (0,)), ((), ())), preferred_eleme...  9.77 us
  transfers between devices with their start and end apart: 5, of which 3 were waited for; matrix products, arithmetic and copies ran while one was open for 11% of the time, Pallas kernels for 0%

profile of v1, /device:TPU:1, one launch (start us, length us, event | category | flops | bytes accessed | tf_op | source)
XLA Modules:
  0.0 412.8 jit_solution(10491689202695144847)
XLA Ops:
  7.2 0.0 copy-start
  7.2 0.0 all-gather.3.cloned.1.call-start
  7.2 1.6 sort.17
  8.9 0.0 copy-done
  8.9 0.6 gather_fusion
  9.5 0.5 broadcast.57
  10.0 0.7 reduce.2
  10.7 0.1 reshape.95
  10.8 10.1 %all_to_all.14 = bf16[4,2,4096]{2,1,0:T(2,128)(2,1)S(1)} all-to-all(bf16[4,2,4096]{2,1,0:T(2,128)(2,1)S(1)} %reshape.95), channel_id=1, replica_groups=mesh['dp'=4,'latent'=32] {'dp'}, dimensions={0} | all-to-all | bytes 131072 | tf_op jit(solution)/shard_map/all_to_all | solution.py:25
  20.9 0.7 reshape.96
  21.6 0.0 all-gather.3.cloned.1.call-update
  22.3 0.6 gather_fusion.1
  23.0 0.6 fusion.25
  23.6 0.7 copy.17
  24.3 3.2 all-to-all-start.1
  27.5 0.0 all-reduce.5.cloned.1.call-start
  27.5 1.3 dynamic-slice
  29.6 1.9 all-to-all-done.1
  31.5 0.1 reduce.1
  31.6 0.2 dynamic-update-slice
  31.8 65.9 %all-reduce = bf16[128]{0:T(256)(128)(2,1)S(1)} all-reduce(bf16[128]{0:T(256)(128)(2,1)S(1)} %dynamic-update-slice), channel_id=2, replica_groups=mesh['dp'=4,'latent'=32] {'latent'}, use_global_device_ids=true, to_apply=%add | all-reduce | flops 128 | bytes 512
  97.7 0.0 all-gather.3.cloned.1.call-done
  97.8 7.3 %multiply_reduce_fusion = (f32[512]{0:T(512)S(1)}, f32[128,512]{1,0:T(8,128)S(1)}) fusion(f32[128]{0:T(128)S(1)} %mul.102, f32[512]{0:T(512)} %param.11, bf16[8192,512]{1,0:T(8,128)(2,1)} %bitcast.33, bf16[128,1,8192]{2,1,0:T(2,128)(2,1)} %all-gather.3.cloned.1.call-done), kind=kOutput, calls=%fused_computation.26 | convolution fusion | flops 1074068992 | bytes 10752512 | tf_op jit(solution)/shard_map/dot_general | solution.py:44
  105.1 6.0 %convolution_convert_fusion = bf16[128,8192]{1,0:T(8,128)(2,1)} fusion(bf16[512,8192]{1,0:T(8,128)(2,1)} %param.12, f32[128,512]{1,0:T(8,128)S(1)} %get-tuple-element.18), kind=kOutput, calls=%fused_computation.6 | convolution fusion | flops 1074921472 | bytes 10747904 | tf_op jit(solution)/shard_map/dot_general | solution.py:48
  111.0 0.0 all-reduce.5.cloned.1.call-update
  111.1 0.0 copy-start.2
  111.1 0.2 reduce-scatter.3.cloned.1.call-start
  111.3 11.3 %convert_multiply_fusion.1 = f32[512,8192]{1,0:T(8,128)} fusion(bf16[512,8192]{1,0:T(8,128)(2,1)} %param.12), kind=kLoop, calls=%fused_computation.3 | loop fusion | flops 8388608 | bytes 25165824 | tf_op jit(solution)/shard_map/square | solution.py:38
  122.6 0.0 copy-done.2
  122.6 6.5 %slice_reduce_fusion.1 = (f32[512]{0:T(512)S(1)}, f32[512]{0:T(512)S(1)}) fusion(f32[512,8192]{1,0:T(8,128)} %convert_multiply_fusion.1), kind=kLoop, calls=%fused_computation.8 | loop fusion | flops 4193280 | bytes 16781312 | tf_op jit(solution)/shard_map/reduce_sum | solution.py:39
  129.2 8.8 %copy.19 = bf16[128,1,8192]{0,2,1:T(8,128)(2,1)S(1)} copy(bf16[128,1,8192]{2,1,0:T(2,128)(2,1)} %all-gather.3.cloned.1.call-done) | data formatting | bytes 4194304 | tf_op jit(solution)/shard_map/dot_general | solution.py:61
  138.0 0.6 multiply_reduce_fusion.2
  138.6 75.9 %all-reduce.5.cloned.1.call-done = bf16[128,8192]{1,0:T(8,128)(2,1)} async-done(((bf16[128,8192]{1,0:T(8,128)(2,1)}), bf16[128,8192]{1,0:T(8,128)(2,1)}) %all-reduce.5.cloned.1.call-update) | async-done | bytes 2097168 | tf_op jit(solution)/shard_map/psum | solution.py:49
  214.5 8.7 %subtract_multiply_fusion = f32[128,8192]{1,0:T(8,128)} fusion(bf16[128,8192]{1,0:T(8,128)(2,1)} %all-reduce.5.cloned.1.call-done, f32[128]{0:T(128)S(1)} %mul.102, f32[8192]{0:T(1024)S(1)} %bitcast.36, bf16[128,1,8192]{2,1,0:T(2,128)(2,1)} %all-gather.3.cloned.1.call-done), kind=kLoop, calls=%fused_computation.12 | loop fusion | flops 5242880 | bytes 8421888 | tf_op jit(solution)/shard_map/mul | solution.py:50
  223.2 15.0 %convolution_convert_fusion.1 = bf16[2,4096,512]{2,1,0:T(8,128)(2,1)} fusion(bf16[2,4096,128]{2,1,0:T(8,128)(2,1)S(1)} %bitcast.34, f32[128,512]{1,0:T(8,128)S(1)} %get-tuple-element.18, bf16[512,8192]{1,0:T(8,128)(2,1)} %param.12, f32[128,8192]{1,0:T(8,128)} %subtract_multiply_fusion, f32[512]{0:T(512)S(1)} %get-tuple-element.12, f32[128]{0:T(128)S(1)} %mul.102), kind=kOutput, calls=%fused_computation.9 | convolution fusion | flops 2153119744 | bytes 23333376 | tf_op jit(solution)/shard_map/dot_general | solution.py:61
  238.2 0.0 reduce-scatter.3.cloned.1.call-update
  238.2 0.0 reduce-scatter.5.cloned.1.call-start
  238.3 9.8 %fusion.1 = bf16[512,8192]{1,0:T(8,128)(2,1)} fusion(bf16[512,8192]{1,0:T(8,128)(2,1)} %param.12, f32[512]{0:T(512)S(1)} %get-tuple-element.14, f32[512]{0:T(512)S(1)} %get-tuple-element.13, pred[8192]{0:T(1024)(128)(4,1)S(1)} %iota_compare_fusion, f32[128,8192]{1,0:T(8,128)} %subtract_multiply_fusion, f32[128,512]{1,0:T(8,128)S(1)} %get-tuple-element.18), kind=kOutput, calls=%fused_computation.5 | convolution fusion | flops 1100087296 | bytes 21245952 | tf_op jit(solution)/shard_map/dot_general | solution.py:65
  248.0 0.0 reduce-scatter.5.cloned.1.call-update
  248.1 1.6 multiply_reduce_fusion.1
  251.0 10.2 %all-reduce.2 = (f32[]{:T(128)}, f32[]{:T(128)}) all-reduce(f32[]{:T(128)} %get-tuple-element.15, f32[]{:T(128)S(6)} %add.90), channel_id=1, replica_groups=mesh['dp'=4,'latent'=32] {'dp'}, use_global_device_ids=true, to_apply=%region_6.7 | all-reduce | flops 2 | bytes 16 | tf_op jit(solution)/shard_map/psum | solution.py:81
  261.2 64.9 %all-reduce.1 = (f32[]{:T(128)}, f32[]{:T(128)}) all-reduce(f32[]{:T(128)} %get-tuple-element.9, f32[]{:T(128)} %get-tuple-element.10), channel_id=1, replica_groups=mesh['dp'=4,'latent'=32] {'latent'}, use_global_device_ids=true, to_apply=%region_7.8 | all-reduce | flops 2 | bytes 16 | tf_op jit(solution)/shard_map/psum | solution.py:81
  327.4 0.0 copy-start.1
  328.1 0.0 reduce-scatter.3.cloned.1.call-done
  328.1 3.3 multiply_convert_fusion.1
  331.5 70.3 %reduce-scatter.5.cloned.1.call-done = bf16[512,2048]{1,0:T(8,128)(2,1)} async-done(((bf16[512,8192]{1,0:T(8,128)(2,1)}), bf16[512,2048]{1,0:T(8,128)(2,1)}) %reduce-scatter.5.cloned.1.call-update) | async-done | bytes 2097168 | tf_op jit(solution)/shard_map/reduce_scatter | solution.py:75
  401.7 3.4 multiply_convert_fusion
  405.2 0.0 copy-done.1
  (8 shorter events, 0.0 us)
Async XLA Ops:
  7.2 1.7 copy-start
  7.2 90.6 %all-gather.3.cloned.1.call-start = ((), (), s32[]{:S(2)}) async-start(), calls=%async_computation.4 | async-start | bytes 4325376 | tf_op jit(solution)/shard_map/all_gather | solution.py:29
  24.3 7.2 %all-to-all-start.1 = ((bf16[4,1,1]{2,1,0:T(2,128)(2,1)}), bf16[4,1,1]{2,1,0:T(2,128)(2,1)S(1)}, u32[]{:S(2)}, u32[]{:S(2)}) async-start(bf16[4,1,1]{2,1,0:T(2,128)(2,1)} %copy.17), calls=%async_computation.1 | async-start | bytes 4096 | tf_op jit(solution)/shard_map/all_to_all | solution.py:26
  27.5 187.0 %all-reduce.5.cloned.1.call-start = ((), (), s32[]{:S(2)}) async-start(), calls=%async_computation.5 | async-start | bytes 4194304 | tf_op jit(solution)/shard_map/psum | solution.py:49
  111.1 11.6 %copy-start.2 = (f32[2,4096]{1,0:T(2,128)S(1)}, f32[2,4096]{1,0:T(2,128)}, u32[]{:S(2)}) copy-start(f32[2,4096]{1,0:T(2,128)} %param.13) | copy-start | bytes 98308
  111.1 217.1 %reduce-scatter.3.cloned.1.call-start = ((), (), s32[]{:S(2)}) async-start(), calls=%async_computation.6 | async-start | bytes 10485760 | tf_op jit(solution)/shard_map/reduce_scatter | solution.py:72
  238.2 163.5 %reduce-scatter.5.cloned.1.call-start = ((), (), s32[]{:S(2)}) async-start(), calls=%async_computation.7 | async-start | bytes 10485760 | tf_op jit(solution)/shard_map/reduce_scatter | solution.py:75
  327.4 77.8 %copy-start.1 = (bf16[5,8192]{1,0:T(8,128)(2,1)S(1)}, bf16[5,8192]{1,0:T(8,128)(2,1)}, u32[]{:S(2)}) copy-start(bf16[5,8192]{1,0:T(8,128)(2,1)} %param.7) | copy-start | bytes 245764
Sparse Core Ops, SparseCore 0:
  21.8 47.3 all-gather.2
  111.2 103.2 all-reduce.4
  238.3 80.7 reduce-scatter.2
  321.5 80.2 reduce-scatter.4
